TPU v7x, 256 devices: a whole 4x4x8 slice. The times are simulated.
256 devices in a mesh: dp: 8 (over y, core), expert: 32 (over x, z).
Axes of the slice: x: 4, y: 4, z: 8, core: 2. Of those that a mesh axis runs over, the one named last changes fastest.
Arguments:
- tokens: bfloat16 [32768, 3072], P(('dp', 'expert')), may hold values from -6 to 6
- cotangent: bfloat16 [32768, 3072], P(('dp', 'expert')), may hold values from -0.3125 to 0.3125
- route_ids: int32 [32768, 2], P(('dp', 'expert')), may hold values from 0 to 7, all different within a row; in each aligned block of 128 rows (0 to 127, 128 to 255, ...) at most 36 rows name the same one
- route_probs: float32 [32768, 2], P(('dp', 'expert')), may hold values from 0.2 to 1
- gate_weight: bfloat16 [3072, 8192], P(None, 'expert'), may hold values from -0.109375 to 0.109375
- up_weight: bfloat16 [3072, 8192], P(None, 'expert'), may hold values from -0.109375 to 0.109375
- down_weight: bfloat16 [8192, 3072], P('expert'), may hold values from -0.0625 to 0.0625
Outputs:
- token_grad: bfloat16 [32768, 3072], P(('dp', 'expert'))
- gate_grad: bfloat16 [3072, 8192], P('dp', 'expert')
- up_grad: bfloat16 [3072, 8192], P('dp', 'expert')
- down_grad: bfloat16 [8192, 3072], P('expert', 'dp')
Inputs may be any that keep to these rules, and one draw needn't show every extreme that they name: `route_ids`: in every block of 128 consecutive tokens (the tokens of one device) at most 36 tokens name any one expert, a bound that some block reaches; a token's 2 ids differ.
All inputs are finite; a program needn't handle non-finite values.
Results may differ from a plain program's by a relative error of at most 0.023.
Values may be sent and summed in bfloat16 or wider, within the bound.
A program may use at most 128 MiB of HBM per device.

v0:
```python
import jax
import jax.numpy as jnp
from jax import lax
from jax.sharding import PartitionSpec as P

CAP = 36


def pick_rows(placer, values):
    return lax.dot_general(
        placer, values, (((0,), (0,)), ((), ())), preferred_element_type=jnp.float32
    ).astype(jnp.bfloat16)


def per_device(tokens, cotangent, route_ids, route_probs, gate_weight, up_weight, down_weight):
    hits = route_ids == 0
    chosen = jnp.any(hits, axis=1).astype(jnp.int32)
    share = jnp.sum(jnp.where(hits, route_probs, 0.0), axis=1)
    slots = jnp.cumsum(chosen) - chosen
    placer_mask = (slots[:, None] == jnp.arange(CAP, dtype=jnp.int32)[None, :]) & (
        chosen[:, None] == 1
    )
    placer = placer_mask.astype(jnp.float32)
    placer_half = placer_mask.astype(jnp.bfloat16)
    local_rows = pick_rows(placer_half, tokens)
    local_cotan = pick_rows(placer_half, cotangent)
    local_shares = jnp.sum(placer * share[:, None], axis=0)
    routed, routed_cotan, routed_shares = (
        lax.all_gather(local_rows, "expert", axis=0, tiled=True),
        lax.all_gather(local_cotan, "expert", axis=0, tiled=True),
        lax.all_gather(local_shares.astype(jnp.bfloat16), "expert", axis=0, tiled=True).astype(
            local_shares.dtype
        ),
    )
    gate_pre = jnp.dot(routed, gate_weight, preferred_element_type=jnp.float32)
    up_pre = jnp.dot(routed, up_weight, preferred_element_type=jnp.float32)
    sigma = jax.nn.sigmoid(gate_pre)
    gate_act = gate_pre * sigma
    hidden = (gate_act * up_pre).astype(jnp.bfloat16)
    gate_pre, up_pre, sigma, gate_act, hidden = (gate_pre, up_pre, sigma, gate_act, hidden)
    scaled = (routed_shares[:, None] * routed_cotan.astype(jnp.float32)).astype(jnp.bfloat16)
    down_part = lax.dot_general(
        hidden, scaled, (((0,), (0,)), ((), ())), preferred_element_type=jnp.float32
    )
    hidden_back = lax.dot_general(
        scaled, down_weight, (((1,), (1,)), ((), ())), preferred_element_type=jnp.float32
    )
    gate_back = (hidden_back * up_pre * sigma * (1.0 + gate_pre * (1.0 - sigma))).astype(
        jnp.bfloat16
    )
    up_back = (hidden_back * gate_act).astype(jnp.bfloat16)
    gate_part = lax.dot_general(
        routed, gate_back, (((0,), (0,)), ((), ())), preferred_element_type=jnp.float32
    )
    up_part = lax.dot_general(
        routed, up_back, (((0,), (0,)), ((), ())), preferred_element_type=jnp.float32
    )
    gate_sum, up_sum, down_sum = (
        lax.psum_scatter(
            gate_part.astype(jnp.bfloat16), "dp", scatter_dimension=0, tiled=True
        ).astype(jnp.float32),
        lax.psum_scatter(
            up_part.astype(jnp.bfloat16), "dp", scatter_dimension=0, tiled=True
        ).astype(jnp.float32),
        lax.psum_scatter(
            down_part.astype(jnp.bfloat16), "dp", scatter_dimension=1, tiled=True
        ).astype(jnp.float32),
    )
    partial_value = lax.dot_general(
        gate_back, gate_weight, (((1,), (1,)), ((), ())), preferred_element_type=jnp.float32
    )
    partial_value = partial_value + lax.dot_general(
        up_back, up_weight, (((1,), (1,)), ((), ())), preferred_element_type=jnp.float32
    )
    returned = lax.psum_scatter(
        partial_value.astype(jnp.bfloat16), "expert", scatter_dimension=0, tiled=True
    ).astype(jnp.float32)
    token_grad = jnp.dot(placer, returned, precision=lax.Precision.HIGHEST).astype(jnp.bfloat16)
    return (
        token_grad,
        gate_sum.astype(jnp.bfloat16),
        up_sum.astype(jnp.bfloat16),
        down_sum.astype(jnp.bfloat16),
    )


def solution(mesh):
    in_specs = (
        P(("dp", "expert"), None),
        P(("dp", "expert"), None),
        P(("dp", "expert"), None),
        P(("dp", "expert"), None),
        P(None, "expert"),
        P(None, "expert"),
        P("expert", None),
    )
    out_specs = (P(("dp", "expert"), None), P("dp", "expert"), P("dp", "expert"), P("expert", "dp"))
    return jax.shard_map(
        per_device, mesh=mesh, in_specs=in_specs, out_specs=out_specs, check_vma=False
    )
```

profile of v0, /device:TPU:2, one launch (start us, length us, event | category | flops | bytes accessed | tf_op | source)
XLA Modules:
  0.0 405.0 jit_solution(14300400901029948780)
XLA Ops:
  7.2 0.0 copy-start
  7.2 0.0 copy-start.9
  7.2 0.0 copy-start.7
  7.2 0.0 copy-start.5
  7.2 0.0 copy-start.8
  7.2 0.0 all-gather.7.cloned.1.call-start
  7.3 0.8 fusion.18
  8.1 0.1 copy.14
  8.2 0.2 reduce-window.8
  8.4 0.1 reduce
  8.5 2.1 fusion.3
  10.6 0.0 all-gather.7.cloned.1.call-update
  10.6 0.0 all-gather.5.cloned.1.call-start
  10.7 0.0 copy-done.5
  10.7 0.9 fusion.2
  11.6 0.0 all-gather.5.cloned.1.call-update
  11.6 0.0 reduce-scatter.12.cloned.1.call-start
  11.7 0.0 copy-done.9
  11.7 0.6 fusion.21
  12.9 0.0 copy-done.7
  13.0 0.0 copy-done.8
  13.0 0.1 select_reduce_fusion
  13.1 0.2 dynamic-update-slice
  13.4 66.5 %all-reduce = bf16[1152]{0:T(1024)(128)(2,1)S(1)} all-reduce(bf16[1152]{0:T(1024)(128)(2,1)S(1)} %dynamic-update-slice), channel_id=1, replica_groups=mesh['dp'=8,'expert'=32] {'expert'}, use_global_device_ids=true, to_apply=%add | all-reduce | flops 1152 | bytes 4608
  79.9 28.5 %all-gather.7.cloned.1.call-done = bf16[32,36,3072]{2,1,0:T(8,128)(2,1)} async-done(((bf16[1,36,3072]{2,1,0:T(8,128)(2,1)}), bf16[32,36,3072]{2,1,0:T(8,128)(2,1)}) %all-gather.7.cloned.1.call-update) | async-done | bytes 7077904 | tf_op jit(solution)/shard_map/all_gather | solution.py:29
  108.4 8.8 %reshape.52 = bf16[1152,3072]{1,0:T(8,128)(2,1)} reshape(bf16[32,36,3072]{2,1,0:T(8,128)(2,1)} %all-gather.7.cloned.1.call-done) | data formatting | bytes 14155776
  117.2 0.0 copy-done
  117.2 0.0 copy-start.1
  117.2 0.0 copy-start.2
  117.2 6.2 %fusion.23 = f32[1152,256]{1,0:T(8,128)} fusion(bf16[1152,3072]{1,0:T(8,128)(2,1)} %reshape.52, bf16[3072,256]{1,0:T(8,128)(2,1)S(1)} %copy-done), kind=kOutput, calls=%fused_computation.37 | convolution fusion | flops 1811939328 | bytes 9830400 | tf_op jit(solution)/shard_map/dot_general | solution.py:35
  123.4 0.0 copy-done.1
  123.4 0.0 copy-done.2
  123.4 3.0 fusion.22
  126.5 76.7 %all-gather.5.cloned.1.call-done = bf16[32,36,3072]{2,1,0:T(8,128)(2,1)} async-done(((bf16[1,36,3072]{2,1,0:T(8,128)(2,1)}), bf16[32,36,3072]{2,1,0:T(8,128)(2,1)}) %all-gather.5.cloned.1.call-update) | async-done | bytes 7077904 | tf_op jit(solution)/shard_map/all_gather | solution.py:30
  203.2 9.8 %reshape.53 = f32[1152,3072]{1,0:T(8,128)} reshape(bf16[32,36,3072]{2,1,0:T(8,128)(2,1)} %all-gather.5.cloned.1.call-done) | data formatting | bytes 21233664 | tf_op jit(solution)/shard_map/convert_element_type | solution.py:41
  213.0 8.2 %convolution_convert_fusion = bf16[256,3072]{1,0:T(8,128)(2,1)S(1)} fusion(f32[1152,256]{1,0:T(8,128)} %fusion.22, f32[1152,256]{1,0:T(8,128)} %fusion.23, f32[1152,3072]{1,0:T(8,128)} %reshape.53, f32[1152]{0:T(1024)S(1)} %convert_element_type.76), kind=kOutput, calls=%fused_computation.3 | convolution fusion | flops 1821573120 | bytes 18092544 | tf_op jit(solution)/shard_map/dot_general | solution.py:42
  221.2 1.6 copy.15
  222.8 0.0 copy-start.4
  222.8 0.0 reduce-scatter.12.cloned.1.call-update
  222.8 0.2 reduce-scatter.8.cloned.1.call-start
  223.1 1.0 copy-done.4
  224.1 9.0 %multiply_convert_fusion.2 = (bf16[1152,256]{1,0:T(8,128)(2,1)}, bf16[1152,256]{1,0:T(8,128)(2,1)S(1)}) fusion(f32[1152,256]{1,0:T(8,128)S(1)} %copy-done.4, f32[1152,256]{1,0:T(8,128)} %fusion.22, bf16[256,3072]{1,0:T(8,128)(2,1)} %param.13, f32[1152,3072]{1,0:T(8,128)} %reshape.53, f32[1152]{0:T(1024)S(1)} %convert_element_type.76), kind=kOutput, calls=%fused_computation.12 | convolution fusion | flops 1822851072 | bytes 19272192 | tf_op jit(solution)/shard_map/dot_general | solution.py:45
  233.1 6.5 %convolution_convert_fusion.2 = bf16[3072,256]{1,0:T(8,128)(2,1)} fusion(bf16[1152,3072]{1,0:T(8,128)(2,1)} %reshape.52, bf16[1152,256]{1,0:T(8,128)(2,1)S(1)} %get-tuple-element.5), kind=kOutput, calls=%fused_computation.5 | convolution fusion | flops 1812725760 | bytes 9240576 | tf_op jit(solution)/shard_map/dot_general | solution.py:52
  239.6 0.0 reduce-scatter.8.cloned.1.call-update
  239.6 0.0 reduce-scatter.10.cloned.1.call-start
  239.6 0.0 copy-start.6
  239.6 7.1 %fusion.24 = f32[1152,3072]{1,0:T(8,128)} fusion(bf16[1152,256]{1,0:T(8,128)(2,1)S(1)} %get-tuple-element.5, bf16[3072,256]{1,0:T(8,128)(2,1)S(1)} %copy-done), kind=kOutput, calls=%fused_computation.38 | convolution fusion | flops 1811939328 | bytes 16318464 | tf_op jit(solution)/shard_map/dot_general | solution.py:69
  246.7 0.0 copy-done.6
  246.7 6.5 %convolution_convert_fusion.1 = bf16[3072,256]{1,0:T(8,128)(2,1)} fusion(bf16[1152,3072]{1,0:T(8,128)(2,1)} %reshape.52, bf16[1152,256]{1,0:T(8,128)(2,1)S(1)} %copy-done.6), kind=kOutput, calls=%fused_computation.4 | convolution fusion | flops 1812725760 | bytes 9240576 | tf_op jit(solution)/shard_map/dot_general | solution.py:55
  253.3 0.0 copy-done.3
  253.3 10.3 %fusion.1 = bf16[1152,3072]{1,0:T(8,128)(2,1)} fusion(f32[1152,3072]{1,0:T(8,128)} %fusion.24, bf16[1152,256]{1,0:T(8,128)(2,1)} %get-tuple-element.4, bf16[3072,256]{1,0:T(8,128)(2,1)S(1)} %copy-done.3), kind=kOutput, calls=%fused_computation.2 | convolution fusion | flops 1819017216 | bytes 23396352 | tf_op jit(solution)/shard_map/dot_general | solution.py:72
  263.5 0.0 reduce-scatter.10.cloned.1.call-update
  263.6 92.1 %fusion = bf16[40,3072]{1,0:T(8,128)(2,1)S(1)} fusion(bf16[1152,3072]{1,0:T(8,128)(2,1)} %fusion.1), kind=kCustom, calls=%all-reduce-scatter | all-reduce-scatter fusion | flops 3932161 | bytes 7324672
  355.7 1.9 collective-permute-start.2
  357.6 5.4 %collective-permute-start.1 = (bf16[40,3072]{1,0:T(8,128)(2,1)S(1)}, bf16[40,3072]{1,0:T(8,128)(2,1)S(1)}, u32[]{:S(2)}, u32[]{:S(2)}) collective-permute-start(bf16[40,3072]{1,0:T(8,128)(2,1)S(1)} %fusion), channel_id=1, source_target_pairs={{0,2},{1,3},{2,4},{3,5},{4,6},{5,7},{6,8},{7,9},{8,10},{9,11},{10,... | collective-permute-start | bytes 737288
  363.1 1.9 collective-permute-start
  365.0 6.0 %collective-permute-start.3 = (bf16[4,3072]{1,0:T(4,128)(2,1)S(1)}, bf16[4,3072]{1,0:T(4,128)(2,1)S(1)}, u32[]{:S(2)}, u32[]{:S(2)}) collective-permute-start(bf16[4,3072]{1,0:T(4,128)(2,1)S(1)} %slice), channel_id=1, source_target_pairs={{0,4},{1,5},{2,6},{3,7},{4,8},{5,9},{6,10},{7,11},{8,12},{9,13},{1... | collective-permute-start | bytes 73736
  371.7 20.6 %collective-permute-done.3 = bf16[4,3072]{1,0:T(4,128)(2,1)S(1)} collective-permute-done((bf16[4,3072]{1,0:T(4,128)(2,1)S(1)}, bf16[4,3072]{1,0:T(4,128)(2,1)S(1)}, u32[]{:S(2)}, u32[]{:S(2)}) %collective-permute-start.3) | collective-permute-done | bytes 24608
  392.3 0.0 collective-permute-done.2
  392.3 0.0 collective-permute-done.1
  392.3 0.0 collective-permute-done
  392.3 3.1 concatenate
  395.4 1.3 convolution_convert_fusion.3
  396.7 1.7 copy.16
  (10 shorter events, 0.1 us)
Async XLA Ops:
  7.2 110.0 %copy-start = (bf16[3072,256]{1,0:T(8,128)(2,1)S(1)}, bf16[3072,256]{1,0:T(8,128)(2,1)}, u32[]{:S(2)}) copy-start(bf16[3072,256]{1,0:T(8,128)(2,1)} %param.11) | copy-start | bytes 4718596
  7.2 4.5 %copy-start.9 = (u32[256]{0:T(256)S(1)}, u32[256]{0:T(256)}, u32[]{:S(2)}) copy-start(u32[256]{0:T(256)} %constant.20) | copy-start | bytes 3076
  7.2 5.7 %copy-start.7 = (s32[128,2]{0,1:T(2,128)S(1)}, s32[128,2]{0,1:T(2,128)}, u32[]{:S(2)}) copy-start(s32[128,2]{0,1:T(2,128)} %param.9) | copy-start | bytes 3076
  7.2 3.5 copy-start.5
  7.2 5.7 %copy-start.8 = (f32[128,2]{0,1:T(2,128)S(1)}, f32[128,2]{0,1:T(2,128)}, u32[]{:S(2)}) copy-start(f32[128,2]{0,1:T(2,128)} %param.10) | copy-start | bytes 3076
  7.2 101.2 %all-gather.7.cloned.1.call-start = ((), (), s32[]{:S(2)}) async-start(), calls=%async_computation.6 | async-start | bytes 8110080 | tf_op jit(solution)/shard_map/all_gather | solution.py:29
  10.6 192.6 %all-gather.5.cloned.1.call-start = ((), (), s32[]{:S(2)}) async-start(), calls=%async_computation.5 | async-start | bytes 8110080 | tf_op jit(solution)/shard_map/all_gather | solution.py:30
  11.6 385.1 %reduce-scatter.12.cloned.1.call-start = ((), (), s32[]{:S(2)}) async-start(), calls=%async_computation.7 | async-start | bytes 1769472
  117.2 6.2 %copy-start.1 = (bf16[1152,3072]{1,0:T(8,128)(2,1)S(1)}, bf16[1152,3072]{1,0:T(8,128)(2,1)}, u32[]{:S(2)}) copy-start(bf16[1152,3072]{1,0:T(8,128)(2,1)} %reshape.52) | copy-start | bytes 21233668
  117.2 6.2 %copy-start.2 = (bf16[3072,256]{1,0:T(8,128)(2,1)S(1)}, bf16[3072,256]{1,0:T(8,128)(2,1)}, u32[]{:S(2)}) copy-start(bf16[3072,256]{1,0:T(8,128)(2,1)} %param.12) | copy-start | bytes 4718596
  222.8 1.3 copy-start.4
  222.8 175.6 %reduce-scatter.8.cloned.1.call-start = ((), (), s32[]{:S(2)}) async-start(), calls=%async_computation.3 | async-start | bytes 1769472 | tf_op jit(solution)/shard_map/reduce_scatter | solution.py:59
  239.6 158.9 %reduce-scatter.10.cloned.1.call-start = ((), (), s32[]{:S(2)}) async-start(), calls=%async_computation.4 | async-start | bytes 1769472 | tf_op jit(solution)/shard_map/reduce_scatter | solution.py:62
  239.6 7.1 %copy-start.6 = (bf16[1152,256]{1,0:T(8,128)(2,1)S(1)}, bf16[1152,256]{1,0:T(8,128)(2,1)}, u32[]{:S(2)}) copy-start(bf16[1152,256]{1,0:T(8,128)(2,1)} %get-tuple-element.4) | copy-start | bytes 1769476
  246.7 6.5 %copy-start.3 = (bf16[3072,256]{1,0:T(8,128)(2,1)S(1)}, bf16[3072,256]{1,0:T(8,128)(2,1)}, u32[]{:S(2)}) copy-start(bf16[3072,256]{1,0:T(8,128)(2,1)} %param.12) | copy-start | bytes 4718596
  355.7 36.6 %collective-permute-start.2 = (bf16[40,3072]{1,0:T(8,128)(2,1)S(1)}, bf16[40,3072]{1,0:T(8,128)(2,1)S(1)}, u32[]{:S(2)}, u32[]{:S(2)}) collective-permute-start(bf16[40,3072]{1,0:T(8,128)(2,1)S(1)} %fusion), channel_id=1, source_target_pairs={{0,3},{1,4},{2,5},{3,6},{4,7},{5,8},{6,9},{7,10},{8,11},{9,12},{10... | collective-permute-start | bytes 737288
  357.6 34.7 %collective-permute-start.1 = (bf16[40,3072]{1,0:T(8,128)(2,1)S(1)}, bf16[40,3072]{1,0:T(8,128)(2,1)S(1)}, u32[]{:S(2)}, u32[]{:S(2)}) collective-permute-start(bf16[40,3072]{1,0:T(8,128)(2,1)S(1)} %fusion), channel_id=1, source_target_pairs={{0,2},{1,3},{2,4},{3,5},{4,6},{5,7},{6,8},{7,9},{8,10},{9,11},{10,... | collective-permute-start | bytes 737288
  363.1 29.3 %collective-permute-start = (bf16[40,3072]{1,0:T(8,128)(2,1)S(1)}, bf16[40,3072]{1,0:T(8,128)(2,1)}, u32[]{:S(2)}, u32[]{:S(2)}) collective-permute-start(bf16[40,3072]{1,0:T(8,128)(2,1)S(1)} %fusion), channel_id=1, source_target_pairs={{0,1},{1,2},{2,3},{3,4},{4,5},{5,6},{6,7},{7,8},{8,9},{9,10},{10,1... | collective-permute-start | bytes 737288
  365.0 27.3 %collective-permute-start.3 = (bf16[4,3072]{1,0:T(4,128)(2,1)S(1)}, bf16[4,3072]{1,0:T(4,128)(2,1)S(1)}, u32[]{:S(2)}, u32[]{:S(2)}) collective-permute-start(bf16[4,3072]{1,0:T(4,128)(2,1)S(1)} %slice), channel_id=1, source_target_pairs={{0,4},{1,5},{2,6},{3,7},{4,8},{5,9},{6,10},{7,11},{8,12},{9,13},{1... | collective-permute-start | bytes 73736
Sparse Core Ops, SparseCore 0:
  11.2 97.2 all-gather.6
  111.0 92.1 all-gather.4
  223.0 33.8 reduce-scatter.11
  259.9 34.9 reduce-scatter.7
  297.9 34.9 reduce-scatter.9
where the time goes:
time: 406 us; the launch traced here: 405 us
  blocking collectives  159 us (39%)
  waiting for transfers between devices  126 us (31%)
  matrix products  61.1 us (15%)
  local copies, waits for them, and re-layouts  27.1 us (7%)
  starting transfers between devices  15.7 us (4%)
  between operations  15.3 us (4%)
    unnamed x2, blocking collectives  159 us
    all_gather x1, waiting for transfers between devices, per_device(): lax.all_gather(local_cotan, 'expert', axis=0, tiled=True)  76.7 us
    all_gather x1, waiting for transfers between devices, per_device(): lax.all_gather(local_rows, 'expert', axis=0, tiled=True)  28.5 us
    unnamed x10, waiting for transfers between devices  20.7 us
    unnamed x28, local copies, waits for them, and re-layouts  17.2 us
    unnamed x5, starting transfers between devices  15.4 us
    dot_general x1, matrix products, per_device(): lax.dot_general(up_back, up_weight, (((1,), (1,)), ((), ())), preferred_e...  10.3 us
    convert_element_type x1, local copies, waits for them, and re-layouts, per_device(): routed_cotan.astype(jnp.float32)  9.83 us
  transfers between devices with their start and end apart: 9, of which 3 were waited for; matrix products, arithmetic and copies ran while one was open for 39% of the time, Pallas kernels for 0%

commit v1 on v0

--- a/solution.py
+++ b/solution.py
@@ -4,6 +4,13 @@
 from jax.sharding import PartitionSpec as P
 
 CAP = 36
+
+
+def exchange_gather(shard, axis, along):
+    size = lax.axis_size(axis)
+    pieces = jnp.stack([shard for _ in range(size)])
+    pieces = lax.all_to_all(pieces, axis, split_axis=0, concat_axis=0)
+    return jnp.concatenate(pieces, axis=along)
 
 
 def pick_rows(placer, values):
@@ -27,7 +34,7 @@
     local_shares = jnp.sum(placer * share[:, None], axis=0)
     routed, routed_cotan, routed_shares = (
         lax.all_gather(local_rows, "expert", axis=0, tiled=True),
-        lax.all_gather(local_cotan, "expert", axis=0, tiled=True),
+        exchange_gather(local_cotan, "expert", 0),
         lax.all_gather(local_shares.astype(jnp.bfloat16), "expert", axis=0, tiled=True).astype(
             local_shares.dtype
         ),

time: 406 us -> 526 us (1.30)
  blocking collectives: 159 us -> 374 us
  waiting for transfers between devices: 126 us -> 19 us
  starting transfers between devices: 15.7 us -> 24.4 us
    unnamed x2, blocking collectives: 159 us -> 374 us
    all_gather x1 -> x0, waiting for transfers between devices: 76.7 us -> none  [per_device(): lax.all_gather(local_cotan, 'expert', axis=0, tiled=True)]
    all_gather x1, waiting for transfers between devices: 28.5 us -> 0.02 us  [per_device(): lax.all_gather(local_rows, 'expert', axis=0, tiled=True)]
    all_to_all x0 -> x1, starting transfers between devices: none -> 11.8 us  [exchange_gather(): pieces = lax.all_to_all(pieces, axis, split_axis=0, concat_axis=0)]
    unnamed x10 -> x9, waiting for transfers between devices: 20.7 us -> 18.9 us
  transfers between devices with their start and end apart: 9 -> 9, of which waited for: 3 -> 1; matrix products, arithmetic and copies ran while one was open for 39% -> 32% of each run, Pallas kernels for 0% -> 0%
where the time goes in v1:
time: 526 us; the launch traced here: 525 us
  blocking collectives  374 us (71%)
  matrix products  60.4 us (11%)
  local copies, waits for them, and re-layouts  31.2 us (6%)
  starting transfers between devices  24.4 us (5%)
  waiting for transfers between devices  19 us (4%)
  between operations  15.3 us (3%)
    unnamed x2, blocking collectives  374 us
    unnamed x9, waiting for transfers between devices  18.9 us
    unnamed x28, local copies, waits for them, and re-layouts  17.2 us
    unnamed x5, starting transfers between devices  12.3 us
    all_to_all x1, starting transfers between devices, exchange_gather(): pieces = lax.all_to_all(pieces, axis, split_axis=0, concat_axis=0)  11.8 us
  transfers between devices with their start and end apart: 9, of which 1 were waited for; matrix products, arithmetic and copies ran while one was open for 32% of the time, Pallas kernels for 0%

profile of v1, /device:TPU:2, one launch (start us, length us, event | category | flops | bytes accessed | tf_op | source)
XLA Modules:
  0.0 525.4 jit_solution(720912404559800143)
XLA Ops:
  7.2 0.0 copy-start
  7.2 0.0 copy-start.5
  7.2 0.0 all-gather.3.cloned.1.call-start
  7.2 0.8 fusion.17
  8.1 0.1 copy.14
  8.2 0.2 reduce-window.8
  8.4 0.1 reduce
  8.5 2.1 fusion.2
  10.6 0.0 all-gather.3.cloned.1.call-update
  10.6 0.0 copy-done.5
  10.6 0.2 convolution_convert_fusion.5
  10.9 4.0 stack.2
  14.9 0.0 copy-start.9
  14.9 0.0 copy-start.7
  14.9 0.0 copy-start.8
  14.9 11.8 %all-to-all-start = ((bf16[32,36,3072]{2,1,0:T(8,128)(2,1)}), bf16[32,36,3072]{2,1,0:T(8,128)(2,1)}, u32[]{:S(2)}, u32[]{:S(2)}) async-start(bf16[32,36,3072]{2,1,0:T(8,128)(2,1)} %stack.2), calls=%async_computation | async-start | bytes 15728640 | tf_op jit(solution)/shard_map/all_to_all | solution.py:12
  26.7 0.0 reduce-scatter.12.cloned.1.call-start
  26.8 0.0 copy-done.9
  26.8 0.6 fusion.20
  28.0 0.0 copy-done.7
  28.0 0.0 copy-done.8
  28.1 0.1 select_reduce_fusion
  28.2 0.2 dynamic-update-slice
  28.4 272.4 %all-reduce = bf16[1152]{0:T(1024)(128)(2,1)S(1)} all-reduce(bf16[1152]{0:T(1024)(128)(2,1)S(1)} %dynamic-update-slice), channel_id=1, replica_groups=mesh['dp'=8,'expert'=32] {'expert'}, use_global_device_ids=true, to_apply=%add | all-reduce | flops 1152 | bytes 4608
  300.9 0.0 all-gather.3.cloned.1.call-done
  300.9 8.8 %reshape.56 = bf16[1152,3072]{1,0:T(8,128)(2,1)} reshape(bf16[32,36,3072]{2,1,0:T(8,128)(2,1)} %all-gather.3.cloned.1.call-done) | data formatting | bytes 14155776
  309.7 0.0 copy-done
  309.7 0.0 copy-start.2
  309.7 6.2 %fusion.22 = f32[1152,256]{1,0:T(8,128)} fusion(bf16[1152,3072]{1,0:T(8,128)(2,1)} %reshape.56, bf16[3072,256]{1,0:T(8,128)(2,1)S(1)} %copy-done), kind=kOutput, calls=%fused_computation.36 | convolution fusion | flops 1811939328 | bytes 9830400 | tf_op jit(solution)/shard_map/dot_general | solution.py:42
  315.9 0.0 copy-done.1
  315.9 0.0 copy-done.2
  315.9 3.0 fusion.21
  318.9 0.0 all-to-all-done
  319.0 9.8 %reshape.51 = f32[1152,3072]{1,0:T(8,128)} reshape(bf16[32,36,3072]{2,1,0:T(8,128)(2,1)} %all-to-all-done) | data formatting | bytes 21233664 | tf_op jit(solution)/shard_map/convert_element_type | solution.py:48
  328.8 8.2 %convolution_convert_fusion = bf16[256,3072]{1,0:T(8,128)(2,1)S(1)} fusion(f32[1152,256]{1,0:T(8,128)} %fusion.21, f32[1152,256]{1,0:T(8,128)} %fusion.22, f32[1152,3072]{1,0:T(8,128)} %reshape.51, f32[1152]{0:T(1024)S(1)} %convert_element_type.79), kind=kOutput, calls=%fused_computation.3 | convolution fusion | flops 1821573120 | bytes 18092544 | tf_op jit(solution)/shard_map/dot_general | solution.py:49
  337.0 1.6 copy.15
  338.6 0.0 copy-start.4
  338.6 0.0 reduce-scatter.12.cloned.1.call-update
  338.6 0.2 reduce-scatter.8.cloned.1.call-start
  338.9 1.0 copy-done.4
  339.9 9.0 %multiply_convert_fusion.2 = (bf16[1152,256]{1,0:T(8,128)(2,1)}, bf16[1152,256]{1,0:T(8,128)(2,1)S(1)}) fusion(f32[1152,256]{1,0:T(8,128)S(1)} %copy-done.4, f32[1152,256]{1,0:T(8,128)} %fusion.21, bf16[256,3072]{1,0:T(8,128)(2,1)} %param.13, f32[1152,3072]{1,0:T(8,128)} %reshape.51, f32[1152]{0:T(1024)S(1)} %convert_element_type.79), kind=kOutput, calls=%fused_computation.11 | convolution fusion | flops 1822851072 | bytes 19272192 | tf_op jit(solution)/shard_map/dot_general | solution.py:52
  348.9 6.5 %convolution_convert_fusion.2 = bf16[3072,256]{1,0:T(8,128)(2,1)} fusion(bf16[1152,3072]{1,0:T(8,128)(2,1)} %reshape.56, bf16[1152,256]{1,0:T(8,128)(2,1)S(1)} %get-tuple-element.5), kind=kOutput, calls=%fused_computation.5 | convolution fusion | flops 1812725760 | bytes 9240576 | tf_op jit(solution)/shard_map/dot_general | solution.py:59
  355.3 0.0 reduce-scatter.8.cloned.1.call-update
  355.4 0.0 reduce-scatter.10.cloned.1.call-start
  355.4 0.0 copy-start.6
  355.4 7.1 %fusion.23 = f32[1152,3072]{1,0:T(8,128)} fusion(bf16[1152,256]{1,0:T(8,128)(2,1)S(1)} %get-tuple-element.5, bf16[3072,256]{1,0:T(8,128)(2,1)S(1)} %copy-done), kind=kOutput, calls=%fused_computation.37 | convolution fusion | flops 1811939328 | bytes 16318464 | tf_op jit(solution)/shard_map/dot_general | solution.py:76
  362.5 0.0 copy-done.6
  362.5 0.0 copy-start.3
  362.5 6.5 %convolution_convert_fusion.1 = bf16[3072,256]{1,0:T(8,128)(2,1)} fusion(bf16[1152,3072]{1,0:T(8,128)(2,1)} %reshape.56, bf16[1152,256]{1,0:T(8,128)(2,1)S(1)} %copy-done.6), kind=kOutput, calls=%fused_computation.4 | convolution fusion | flops 1812725760 | bytes 9240576 | tf_op jit(solution)/shard_map/dot_general | solution.py:62
  369.0 0.0 copy-done.3
  369.0 10.3 %fusion.1 = bf16[1152,3072]{1,0:T(8,128)(2,1)} fusion(f32[1152,3072]{1,0:T(8,128)} %fusion.23, bf16[1152,256]{1,0:T(8,128)(2,1)} %get-tuple-element.4, bf16[3072,256]{1,0:T(8,128)(2,1)S(1)} %copy-done.3), kind=kOutput, calls=%fused_computation.2 | convolution fusion | flops 1819017216 | bytes 23396352 | tf_op jit(solution)/shard_map/dot_general | solution.py:79
  379.3 0.0 reduce-scatter.10.cloned.1.call-update
  379.4 101.5 %fusion = bf16[40,3072]{1,0:T(8,128)(2,1)S(1)} fusion(bf16[1152,3072]{1,0:T(8,128)(2,1)} %fusion.1), kind=kCustom, calls=%all-reduce-scatter | all-reduce-scatter fusion | flops 3932161 | bytes 7324672
  480.8 1.9 collective-permute-start.2
  482.8 1.9 collective-permute-start.1
  484.7 1.9 collective-permute-start
  486.7 6.5 %collective-permute-start.3 = (bf16[4,3072]{1,0:T(4,128)(2,1)S(1)}, bf16[4,3072]{1,0:T(4,128)(2,1)S(1)}, u32[]{:S(2)}, u32[]{:S(2)}) collective-permute-start(bf16[4,3072]{1,0:T(4,128)(2,1)S(1)} %slice), channel_id=1, source_target_pairs={{0,4},{1,5},{2,6},{3,7},{4,8},{5,9},{6,10},{7,11},{8,12},{9,13},{1... | collective-permute-start | bytes 73736
  493.8 18.9 %collective-permute-done.3 = bf16[4,3072]{1,0:T(4,128)(2,1)S(1)} collective-permute-done((bf16[4,3072]{1,0:T(4,128)(2,1)S(1)}, bf16[4,3072]{1,0:T(4,128)(2,1)S(1)}, u32[]{:S(2)}, u32[]{:S(2)}) %collective-permute-start.3) | collective-permute-done | bytes 24608
  512.7 0.0 collective-permute-done.2
  512.7 0.0 collective-permute-done.1
  512.7 0.0 collective-permute-done
  512.7 3.1 concatenate
  515.8 1.3 convolution_convert_fusion.3
  517.1 1.7 copy.16
  (10 shorter events, 0.1 us)
Async XLA Ops:
  7.2 302.5 %copy-start = (bf16[3072,256]{1,0:T(8,128)(2,1)S(1)}, bf16[3072,256]{1,0:T(8,128)(2,1)}, u32[]{:S(2)}) copy-start(bf16[3072,256]{1,0:T(8,128)(2,1)} %param.11) | copy-start | bytes 4718596
  7.2 3.4 copy-start.5
  7.2 293.7 %all-gather.3.cloned.1.call-start = ((), (), s32[]{:S(2)}) async-start(), calls=%async_computation.6 | async-start | bytes 8110080 | tf_op jit(solution)/shard_map/all_gather | solution.py:36
  14.9 11.9 %copy-start.9 = (u32[256]{0:T(256)S(1)}, u32[256]{0:T(256)}, u32[]{:S(2)}) copy-start(u32[256]{0:T(256)} %constant.20) | copy-start | bytes 3076
  14.9 13.1 %copy-start.7 = (s32[128,2]{0,1:T(2,128)S(1)}, s32[128,2]{0,1:T(2,128)}, u32[]{:S(2)}) copy-start(s32[128,2]{0,1:T(2,128)} %param.9) | copy-start | bytes 3076
  14.9 13.1 %copy-start.8 = (f32[128,2]{0,1:T(2,128)S(1)}, f32[128,2]{0,1:T(2,128)}, u32[]{:S(2)}) copy-start(f32[128,2]{0,1:T(2,128)} %param.10) | copy-start | bytes 3076
  14.9 304.1 %all-to-all-start = ((bf16[32,36,3072]{2,1,0:T(8,128)(2,1)}), bf16[32,36,3072]{2,1,0:T(8,128)(2,1)}, u32[]{:S(2)}, u32[]{:S(2)}) async-start(bf16[32,36,3072]{2,1,0:T(8,128)(2,1)} %stack.2), calls=%async_computation | async-start | bytes 15728640 | tf_op jit(solution)/shard_map/all_to_all | solution.py:12
  26.7 490.4 %reduce-scatter.12.cloned.1.call-start = ((), (), s32[]{:S(2)}) async-start(), calls=%async_computation.7 | async-start | bytes 1769472
  309.7 6.2 %copy-start.1 = (bf16[1152,3072]{1,0:T(8,128)(2,1)S(1)}, bf16[1152,3072]{1,0:T(8,128)(2,1)}, u32[]{:S(2)}) copy-start(bf16[1152,3072]{1,0:T(8,128)(2,1)} %reshape.56) | copy-start | bytes 21233668
  309.7 6.2 %copy-start.2 = (bf16[3072,256]{1,0:T(8,128)(2,1)S(1)}, bf16[3072,256]{1,0:T(8,128)(2,1)}, u32[]{:S(2)}) copy-start(bf16[3072,256]{1,0:T(8,128)(2,1)} %param.12) | copy-start | bytes 4718596
  338.6 1.3 copy-start.4
  338.6 180.2 %reduce-scatter.8.cloned.1.call-start = ((), (), s32[]{:S(2)}) async-start(), calls=%async_computation.4 | async-start | bytes 1769472 | tf_op jit(solution)/shard_map/reduce_scatter | solution.py:66
  355.4 163.5 %reduce-scatter.10.cloned.1.call-start = ((), (), s32[]{:S(2)}) async-start(), calls=%async_computation.5 | async-start | bytes 1769472 | tf_op jit(solution)/shard_map/reduce_scatter | solution.py:69
  355.4 7.1 %copy-start.6 = (bf16[1152,256]{1,0:T(8,128)(2,1)S(1)}, bf16[1152,256]{1,0:T(8,128)(2,1)}, u32[]{:S(2)}) copy-start(bf16[1152,256]{1,0:T(8,128)(2,1)} %get-tuple-element.4) | copy-start | bytes 1769476
  362.5 6.5 %copy-start.3 = (bf16[3072,256]{1,0:T(8,128)(2,1)S(1)}, bf16[3072,256]{1,0:T(8,128)(2,1)}, u32[]{:S(2)}) copy-start(bf16[3072,256]{1,0:T(8,128)(2,1)} %param.12) | copy-start | bytes 4718596
  480.8 31.9 %collective-permute-start.2 = (bf16[40,3072]{1,0:T(8,128)(2,1)S(1)}, bf16[40,3072]{1,0:T(8,128)(2,1)S(1)}, u32[]{:S(2)}, u32[]{:S(2)}) collective-permute-start(bf16[40,3072]{1,0:T(8,128)(2,1)S(1)} %fusion), channel_id=1, source_target_pairs={{0,3},{1,4},{2,5},{3,6},{4,7},{5,8},{6,9},{7,10},{8,11},{9,12},{10... | collective-permute-start | bytes 737288
  482.8 29.9 %collective-permute-start.1 = (bf16[40,3072]{1,0:T(8,128)(2,1)S(1)}, bf16[40,3072]{1,0:T(8,128)(2,1)S(1)}, u32[]{:S(2)}, u32[]{:S(2)}) collective-permute-start(bf16[40,3072]{1,0:T(8,128)(2,1)S(1)} %fusion), channel_id=1, source_target_pairs={{0,2},{1,3},{2,4},{3,5},{4,6},{5,7},{6,8},{7,9},{8,10},{9,11},{10,... | collective-permute-start | bytes 737288
  484.7 28.0 %collective-permute-start = (bf16[40,3072]{1,0:T(8,128)(2,1)S(1)}, bf16[40,3072]{1,0:T(8,128)(2,1)}, u32[]{:S(2)}, u32[]{:S(2)}) collective-permute-start(bf16[40,3072]{1,0:T(8,128)(2,1)S(1)} %fusion), channel_id=1, source_target_pairs={{0,1},{1,2},{2,3},{3,4},{4,5},{5,6},{6,7},{7,8},{8,9},{9,10},{10,1... | collective-permute-start | bytes 737288
  486.7 26.0 %collective-permute-start.3 = (bf16[4,3072]{1,0:T(4,128)(2,1)S(1)}, bf16[4,3072]{1,0:T(4,128)(2,1)S(1)}, u32[]{:S(2)}, u32[]{:S(2)}) collective-permute-start(bf16[4,3072]{1,0:T(4,128)(2,1)S(1)} %slice), channel_id=1, source_target_pairs={{0,4},{1,5},{2,6},{3,7},{4,8},{5,9},{6,10},{7,11},{8,12},{9,13},{1... | collective-permute-start | bytes 73736
Sparse Core Ops, SparseCore 0:
  11.1 201.3 all-gather.2
  338.8 39.8 reduce-scatter.11
  381.8 35.0 reduce-scatter.7
  419.9 34.9 reduce-scatter.9
